TPU v7x, 256 devices: a whole 4x4x8 slice. The times are simulated.
256 devices in a mesh: band: 16 (over z, y_lo), col: 16 (over x, y_hi, core).
Axes of the slice: x: 4, y: 4 (y_hi: 2, y_lo: 2; y = y_hi * 2 + y_lo), z: 8, core: 2. Of those that a mesh axis runs over, the one named last changes fastest.
Arguments:
- valence_wave: bfloat16 [16, 96, 9216], P('band', 'col'), may hold values from -6 to 6
- conduction_wave: bfloat16 [16, 96, 9216], P('band', 'col'), may hold values from -6 to 6
- valence_index: int32 [16], replicated, may hold values from 0 to 4095
- occupied_energy: float32 [4096], replicated, may hold values from -6 to -0.5
- conduction_energy: float32 [16], replicated, may hold values from 0.5 to 8
- frequency: float32 [4], replicated, may hold values from 0.5 to 16
- gvec_cell: int32 [32768], P('col'), may hold values from 0 to 55295, as said below
- block_cell: int32 [16], P('col'), may hold values from 0 to 55295, as said below
Outputs:
- chi: float32 [32768, 128], P(('col', 'band'))
Inputs may be any that keep to these rules, and one draw needn't show every extreme that they name: `gvec_cell`: for rows j of owner k (k * 2048 <= j < (k + 1) * 2048) the entry is (kx 6 + ky - k * 6) * 96 + kz for the G vector's grid point (kx, ky, kz), whose ky lies in [k * 6, (k + 1) * 6); no point appears twice among the rows and block columns of one owner. `block_cell`: block column m has owner k = m // 1 and is encoded as for gvec_cell; its points differ from every row point of the same owner.
All inputs are finite; a program needn't handle non-finite values.
Results may differ from a plain program's by a relative error of at most 0.018.
Values may be sent and summed in bfloat16 or wider, within the bound.
No kernel may reach another device: no remote copies, remote signals or barrier semaphores. Data moves between devices by JAX's collectives and lax.ppermute only.
A program may use at most 128 MiB of HBM per device.

v0:
```python
import math
import jax
import jax.numpy as jnp
from jax import lax
from jax.sharding import PartitionSpec as P

GY = 96


def joined_along(pieces, dim):
    dims = list(pieces.shape[1:])
    dims[dim] *= pieces.shape[0]
    return jnp.moveaxis(pieces, 0, dim).reshape(dims)


def copy_for_each(x, axis):
    devices = lax.axis_size(axis)
    return lax.all_to_all(jnp.broadcast_to(x[None], (devices, *x.shape)), axis, 0, 0, tiled=True)


def collect(x, axis, dim):
    return joined_along(copy_for_each(x, axis), dim)


def cut_along(x, dim, devices):
    dims = x.shape
    pieces = x.reshape(*dims[:dim], devices, dims[dim] // devices, *dims[dim + 1 :])
    return jnp.moveaxis(pieces, dim, 0)


def sent_and_summed(x, axis, dim):
    pieces = cut_along(x, dim, lax.axis_size(axis))
    arrived = lax.all_to_all(pieces, axis, split_axis=0, concat_axis=0, tiled=True)
    return arrived.astype(jnp.float32).sum(axis=0)


def dft_tables(length, factor, out_type):
    indices = jnp.arange(length, dtype=jnp.int32)
    phases = indices[:, None] * indices[None, :] % length
    angles = phases.astype(jnp.float32) * (2.0 * math.pi / length)
    return (
        (jnp.cos(angles) * factor).astype(out_type),
        (-jnp.sin(angles) * factor).astype(out_type),
    )


def weighted_columns(block, weights):
    columns = block.astype(jnp.float32)
    stacked = jnp.stack([columns, jnp.stack([-columns[1], columns[0]])])
    scaled = stacked[None] * weights[:, None, None, :, None]
    scaled = scaled.transpose(2, 3, 0, 1, 4).astype(jnp.bfloat16)
    return scaled.reshape(2, block.shape[1], -1)


def pair_weights(
    pair_ids, valence_energy, conduction_energy, frequency, per_band, pairs_dev, norm_factor
):
    band_of = pair_ids // pairs_dev
    within = pair_ids % pairs_dev
    valence_of = within // per_band
    conduction_of = band_of * per_band + within % per_band
    valence_range = jnp.arange(valence_energy.shape[0], dtype=jnp.int32)
    conduction_range = jnp.arange(conduction_energy.shape[0], dtype=jnp.int32)
    valence_pick = jnp.sum(
        jnp.where(valence_of[:, None] == valence_range[None, :], valence_energy[None, :], 0.0),
        axis=1,
    )
    conduction_pick = jnp.sum(
        jnp.where(
            conduction_of[:, None] == conduction_range[None, :], conduction_energy[None, :], 0.0
        ),
        axis=1,
    )
    gap = conduction_pick - valence_pick
    freq_column = frequency[:, None]
    return (
        -4.0
        * gap[None, :]
        / (gap[None, :] * gap[None, :] + freq_column * freq_column)
        * norm_factor
    )


def per_device(
    valence_wave,
    conduction_wave,
    valence_index,
    occupied_energy,
    conduction_energy,
    frequency,
    gvec_cell,
    block_cell,
):
    local_valence, slab_x, plane_size = valence_wave.shape
    per_band = conduction_wave.shape[0]
    band_count = lax.axis_size("band")
    col_count = lax.axis_size("col")
    grid_x = slab_x * col_count
    grid_y = GY
    grid_z = plane_size // grid_y
    total_valence = local_valence * band_count
    pairs_dev = total_valence * per_band
    total_conduction = conduction_energy.shape[0]
    norm_factor = 1.0 / math.sqrt(total_valence * total_conduction)
    high = lax.Precision.HIGH
    z_cosine, z_sine = dft_tables(grid_z, 1.0, jnp.float32)
    y_cosine, y_sine = dft_tables(grid_y, 1.0 / math.sqrt(grid_y * grid_z), jnp.float32)
    x_cosine, x_sine = dft_tables(grid_x, 1.0 / math.sqrt(grid_x), jnp.bfloat16)
    x_table = jnp.stack([jnp.stack([x_cosine, -x_sine]), jnp.stack([x_sine, x_cosine])])
    conduction_float = conduction_wave.astype(jnp.float32)
    products = (
        collect(valence_wave, "band", 0).astype(jnp.float32)[:, None] * conduction_float[None]
    )
    products = products.reshape(-1, slab_x, grid_y, grid_z)
    z_real = jnp.einsum("kz,pxyz->pxyk", z_cosine, products, precision=high)
    z_imag = jnp.einsum("kz,pxyz->pxyk", z_sine, products, precision=high)
    y_real = jnp.einsum("jy,pxyk->pxjk", y_cosine, z_real, precision=high) - jnp.einsum(
        "jy,pxyk->pxjk", y_sine, z_imag, precision=high
    )
    y_imag = jnp.einsum("jy,pxyk->pxjk", y_sine, z_real, precision=high) + jnp.einsum(
        "jy,pxyk->pxjk", y_cosine, z_imag, precision=high
    )
    planes = jnp.stack([y_real, y_imag]).astype(jnp.bfloat16)
    exchanged = lax.all_to_all(planes, "col", split_axis=3, concat_axis=2, tiled=True)
    items = exchanged.shape[1]
    flat = exchanged.reshape(2, items, grid_x, -1)
    density = jnp.einsum(
        "orkx,rpxf->opkf", x_table, flat, preferred_element_type=jnp.float32
    ).astype(jnp.bfloat16)
    density = density.reshape(2, items, -1)
    row_density = jnp.take(density, gvec_cell, axis=2)
    block_density = jnp.take(density, block_cell, axis=2)
    block_all = collect(block_density, "col", 2)
    occupied_range = jnp.arange(occupied_energy.shape[0], dtype=jnp.int32)
    valence_energy = jnp.sum(
        jnp.where(valence_index[:, None] == occupied_range[None, :], occupied_energy[None, :], 0.0),
        axis=1,
    )
    pair_ids = lax.axis_index("band") * pairs_dev + jnp.arange(pairs_dev, dtype=jnp.int32)
    weights = pair_weights(
        pair_ids, valence_energy, conduction_energy, frequency, per_band, pairs_dev, norm_factor
    )
    right_side = weighted_columns(block_all, weights)
    return sent_and_summed(
        jnp.einsum(
            "rpg,rpc->gc", row_density, right_side, preferred_element_type=jnp.float32
        ).astype(jnp.bfloat16),
        "band",
        0,
    )


def solution(mesh):
    return jax.shard_map(
        per_device,
        mesh=mesh,
        in_specs=(
            P("band", "col", None),
            P("band", "col", None),
            P(),
            P(),
            P(),
            P(),
            P("col"),
            P("col"),
        ),
        out_specs=P(("col", "band"), None),
        check_vma=False,
    )
```

profile of v0, /device:TPU:2, one launch (start us, length us, event | category | flops | bytes accessed | tf_op | source)
XLA Modules:
  0.0 309.4 jit_solution(16333228598212090025)
XLA Ops:
  0.0 0.0 copy-start.1
  0.0 2.6 broadcast_in_dim.93
  2.6 9.6 %all-to-all-start = ((bf16[16,1,6,9216]{3,2,1,0:T(8,128)(2,1)}), bf16[16,1,6,9216]{3,2,1,0:T(8,128)(2,1)S(1)}, u32[]{:S(2)}, u32[]{:S(2)}) async-start(bf16[16,1,6,9216]{3,2,1,0:T(8,128)(2,1)} %broadcast_in_dim.93), calls=%async_computation | async-start | bytes 4718592 | tf_op jit(solution)/shard_map/all_to_all | solution.py:18
  12.2 0.0 copy-done.1
  12.2 55.8 %all-to-all-done = bf16[16,1,6,9216]{3,2,1,0:T(8,128)(2,1)S(1)} async-done(((bf16[16,1,6,9216]{3,2,1,0:T(8,128)(2,1)}), bf16[16,1,6,9216]{3,2,1,0:T(8,128)(2,1)S(1)}, u32[]{:S(2)}, u32[]{:S(2)}) %all-to-all-start) | async-done | bytes 1769504 | tf_op jit(solution)/shard_map/all_to_all | solution.py:18
  68.0 2.6 convert_multiply_fusion
  70.6 5.9 %reshape.293 = f32[16,6,96,96]{3,2,1,0:T(8,128)} reshape(f32[16,1,6,9216]{3,2,1,0:T(8,128)} %convert_multiply_fusion) | data formatting | bytes 7077888 | tf_op jit(solution)/shard_map/reshape | solution.py:114
  76.5 0.0 copy-start
  76.5 7.9 %fusion.18 = f32[16,6,96,96]{2,3,1,0:T(8,128)S(1)} fusion(f32[16,6,96,96]{3,2,1,0:T(8,128)} %reshape.293), kind=kOutput, calls=%fused_computation.33 | convolution fusion | flops 509690880 | bytes 7077888 | tf_op jit(solution)/shard_map/kz,pxyz->pxyk/dot_general | solution.py:115
  84.4 0.0 copy-done
  84.4 5.4 %fusion.16 = f32[16,6,96,96]{2,3,1,0:T(8,128)S(1)} fusion(f32[16,6,96,96]{3,2,1,0:T(8,128)S(1)} %copy-done), kind=kOutput, calls=%fused_computation.31 | convolution fusion | flops 509700096 | bytes 7077888 | tf_op jit(solution)/shard_map/kz,pxyz->pxyk/dot_general | solution.py:116
  89.8 2.3 fusion.23
  92.1 2.2 fusion.21
  94.3 2.9 fusion.7
  97.2 2.7 fusion.6
  100.0 3.2 %pad_maximum_fusion = bf16[2,16,6,96,96]{3,4,2,1,0:T(8,128)(2,1)} fusion(bf16[1,16,6,96,96]{3,4,2,1,0:T(8,128)(2,1)S(1)} %fusion.7, bf16[1,16,6,96,96]{3,4,2,1,0:T(8,128)(2,1)S(1)} %fusion.6), kind=kLoop, calls=%fused_computation.2 | loop fusion | flops 1769472 | bytes 7077888 | tf_op jit(solution)/shard_map/stack | solution.py:123
  103.2 9.2 %copy.84 = bf16[2,16,6,96,96]{4,1,2,0,3:T(8,128)(2,1)} copy(bf16[2,16,6,96,96]{3,4,2,1,0:T(8,128)(2,1)} %pad_maximum_fusion) | data formatting | bytes 7077888 | tf_op jit(solution)/shard_map/stack | solution.py:123
  112.4 0.0 copy-start.5
  112.4 0.0 copy-start.6
  112.4 0.0 copy-start.3
  112.4 0.0 copy-start.4
  112.4 0.0 copy-start.2
  112.4 7.3 %all-to-all-start.1 = ((bf16[2,16,6,96,96]{4,1,2,0,3:T(8,128)(2,1)}), bf16[2,16,6,96,96]{4,1,2,0,3:T(8,128)(2,1)}, u32[]{:S(2)}, u32[]{:S(2)}) async-start(bf16[2,16,6,96,96]{4,1,2,0,3:T(8,128)(2,1)} %copy.84), calls=%async_computation.1 | async-start | bytes 9437184 | tf_op jit(solution)/shard_map/all_to_all | solution.py:124
  120.4 0.0 copy-done.5
  120.4 0.0 copy-done.6
  120.4 0.2 select_reduce_fusion.2
  120.6 0.0 copy-done.3
  120.6 0.0 copy-done.4
  120.6 0.2 select_reduce_fusion
  120.9 0.2 select_reduce_fusion.1
  121.0 0.1 divide_multiply_fusion
  121.1 0.1 mul.268
  121.3 0.1 mul.269
  121.4 0.2 fusion.62
  121.6 0.2 multiply_convert_fusion
  121.9 0.0 copy-done.2
  121.9 53.6 %all-to-all-done.1 = bf16[2,16,6,96,96]{4,1,2,0,3:T(8,128)(2,1)} async-done(((bf16[2,16,6,96,96]{4,1,2,0,3:T(8,128)(2,1)}), bf16[2,16,6,96,96]{4,1,2,0,3:T(8,128)(2,1)}, u32[]{:S(2)}, u32[]{:S(2)}) %all-to-all-start.1) | async-done | bytes 3538976 | tf_op jit(solution)/shard_map/all_to_all | solution.py:124
  175.5 8.2 %copy.102 = bf16[2,16,16,6,6,96]{5,4,3,2,0,1:T(8,128)(2,1)} copy(bf16[2,16,16,6,6,96]{5,1,3,0,4,2:T(8,128)(2,1)} %bitcast.18) | data formatting | bytes 7077888 | tf_op jit(solution)/shard_map/reshape | solution.py:126
  183.8 9.6 %reshape.287 = bf16[2,16,96,576,1]{3,2,0,1,4:T(8,128)(2,1)} reshape(bf16[2,16,16,6,6,96]{5,4,3,2,0,1:T(8,128)(2,1)} %copy.102) | data formatting | bytes 7077888 | tf_op jit(solution)/shard_map/reshape | solution.py:126
  193.4 5.3 %fusion = bf16[2,16,96,576]{3,2,0,1:T(8,128)(2,1)} fusion(bf16[2,16,96,576,1]{3,2,0,1,4:T(8,128)(2,1)} %reshape.287, bf16[1,2,96,96]{3,2,1,0:T(8,128)(2,1)S(1)} %get-tuple-element.17, bf16[1,2,96,96]{3,2,1,0:T(8,128)(2,1)S(1)} %get-tuple-element.16), kind=kOutput, calls=%fused_computation.6 | convolution fusion | flops 681394176 | bytes 7151616 | tf_op jit(solution)/shard_map/orkx,rpxf->opkf/dot_general | solution.py:127
  198.7 44.3 %copy.105 = bf16[2,16,96,576]{1,0,3,2:T(2,128)(2,1)} copy(bf16[2,16,96,576]{3,2,0,1:T(8,128)(2,1)} %fusion) | data formatting | bytes 7077888 | tf_op jit(solution)/shard_map/reshape | solution.py:130
  243.0 16.1 %gather_fusion = bf16[2048,2,16]{2,1,0:T(2,128)(2,1)S(1)} fusion(bf16[2,16,55296]{1,0,2:T(2,128)(2,1)} %bitcast.91, s32[2048]{0:T(1024)S(1)} %fusion.65), kind=kCustom, calls=%fused_computation | custom fusion | bytes 270336 | tf_op jit(solution)/shard_map/jit(_take)/gather | solution.py:131
  259.1 0.7 fusion.66
  259.7 0.6 broadcast_in_dim.99
  260.4 18.7 %all-to-all-start.2 = ((bf16[16,2,16,1]{2,1,3,0:T(2,128)(2,1)}), bf16[16,2,16,1]{2,1,3,0:T(2,128)(2,1)S(1)}, u32[]{:S(2)}, u32[]{:S(2)}) async-start(bf16[16,2,16,1]{2,1,3,0:T(2,128)(2,1)} %broadcast_in_dim.99), calls=%async_computation.2 | async-start | bytes 16384 | tf_op jit(solution)/shard_map/all_to_all | solution.py:18
  279.0 7.4 %fusion.9 = bf16[2,16,2048]{1,0,2:T(2,128)(2,1)S(1)} fusion(bf16[2048,2,16]{2,1,0:T(2,128)(2,1)S(1)} %gather_fusion, pred[2048]{0:T(1024)(128)(4,1)S(1)} %compare_and_fusion), kind=kLoop, calls=%fused_computation.16 | loop fusion | flops 65536 | bytes 264192 | tf_op jit(solution)/shard_map/jit(_take)/select_n | solution.py:131
  286.5 0.0 all-to-all-done.2
  286.5 0.1 copy.90
  286.7 0.2 mul.261
  286.9 0.4 fusion.5
  287.2 21.5 %all_to_all.30 = bf16[16,128,128]{2,1,0:T(8,128)(2,1)S(1)} all-to-all(bf16[16,128,128]{2,1,0:T(8,128)(2,1)S(1)} %bitcast.93), channel_id=1, replica_groups=mesh['band'=16,'col'=16] {'band'}, dimensions={0} | all-to-all | bytes 1048576 | tf_op jit(solution)/shard_map/all_to_all | solution.py:33
  308.7 0.7 convert_reduce_fusion
  (13 shorter events, 0.2 us)
Async XLA Ops:
  0.0 12.2 %copy-start.1 = (bf16[1,6,9216]{2,1,0:T(8,128)(2,1)S(1)}, bf16[1,6,9216]{2,1,0:T(8,128)(2,1)}, u32[]{:S(2)}) copy-start(bf16[1,6,9216]{2,1,0:T(8,128)(2,1)} %param.9) | copy-start | bytes 331780
  2.6 65.4 %all-to-all-start = ((bf16[16,1,6,9216]{3,2,1,0:T(8,128)(2,1)}), bf16[16,1,6,9216]{3,2,1,0:T(8,128)(2,1)S(1)}, u32[]{:S(2)}, u32[]{:S(2)}) async-start(bf16[16,1,6,9216]{3,2,1,0:T(8,128)(2,1)} %broadcast_in_dim.93), calls=%async_computation | async-start | bytes 4718592 | tf_op jit(solution)/shard_map/all_to_all | solution.py:18
  76.5 7.9 %copy-start = (f32[16,6,96,96]{3,2,1,0:T(8,128)S(1)}, f32[16,6,96,96]{3,2,1,0:T(8,128)}, u32[]{:S(2)}) copy-start(f32[16,6,96,96]{3,2,1,0:T(8,128)} %reshape.293) | copy-start | bytes 10616836
  112.4 8.0 %copy-start.5 = (f32[4]{0:T(128)S(1)}, f32[4]{0:T(128)}, u32[]{:S(2)}) copy-start(f32[4]{0:T(128)} %param.13) | copy-start | bytes 52
  112.4 8.1 %copy-start.6 = (f32[16]{0:T(128)S(1)}, f32[16]{0:T(128)}, u32[]{:S(2)}) copy-start(f32[16]{0:T(128)} %param.12) | copy-start | bytes 196
  112.4 8.3 %copy-start.3 = (f32[4096]{0:T(1024)S(1)}, f32[4096]{0:T(1024)}, u32[]{:S(2)}) copy-start(f32[4096]{0:T(1024)} %param.11) | copy-start | bytes 49156
  112.4 8.3 %copy-start.4 = (s32[16]{0:T(128)S(1)}, s32[16]{0:T(128)}, u32[]{:S(2)}) copy-start(s32[16]{0:T(128)} %param.10) | copy-start | bytes 196
  112.4 9.5 %copy-start.2 = (s32[2048]{0:T(1024)S(1)}, s32[2048]{0:T(1024)}, u32[]{:S(2)}) copy-start(s32[2048]{0:T(1024)} %param.14) | copy-start | bytes 24580
  112.4 63.2 %all-to-all-start.1 = ((bf16[2,16,6,96,96]{4,1,2,0,3:T(8,128)(2,1)}), bf16[2,16,6,96,96]{4,1,2,0,3:T(8,128)(2,1)}, u32[]{:S(2)}, u32[]{:S(2)}) async-start(bf16[2,16,6,96,96]{4,1,2,0,3:T(8,128)(2,1)} %copy.84), calls=%async_computation.1 | async-start | bytes 9437184 | tf_op jit(solution)/shard_map/all_to_all | solution.py:124
  260.4 26.1 %all-to-all-start.2 = ((bf16[16,2,16,1]{2,1,3,0:T(2,128)(2,1)}), bf16[16,2,16,1]{2,1,3,0:T(2,128)(2,1)S(1)}, u32[]{:S(2)}, u32[]{:S(2)}) async-start(bf16[16,2,16,1]{2,1,3,0:T(2,128)(2,1)} %broadcast_in_dim.99), calls=%async_computation.2 | async-start | bytes 16384 | tf_op jit(solution)/shard_map/all_to_all | solution.py:18
where the time goes:
time: 313 us; the launch traced here: 309 us
  waiting for transfers between devices  109 us (35%)
  local copies, waits for them, and re-layouts  97.1 us (31%)
  starting transfers between devices  35.6 us (11%)
  matrix products  29.1 us (9%)
  blocking collectives  21.5 us (7%)
  other arithmetic  15.8 us (5%)
    all_to_all x2, waiting for transfers between devices, copy_for_each(): lax.all_to_all(jnp.broadcast_to(x[None], (devices, *x.shape)), axis, 0, 0...  55.8 us
    all_to_all x1, waiting for transfers between devices, per_device(): lax.all_to_all(planes, 'col', split_axis=3, concat_axis=2, tiled=True)  53.6 us
    reshape x1, local copies, waits for them, and re-layouts, per_device(): density = density.reshape(2, items, -1)  44.3 us
    all_to_all x2, starting transfers between devices, copy_for_each(): lax.all_to_all(jnp.broadcast_to(x[None], (devices, *x.shape)), axis, 0, 0...  28.2 us
    all_to_all x1, blocking collectives, sent_and_summed(): lax.all_to_all(pieces, axis, split_axis=0, concat_axis=0, tiled=True)  21.5 us
    reshape x2, local copies, waits for them, and re-layouts, per_device(): flat = exchanged.reshape(2, items, grid_x, -1)  17.8 us
    gather x1, local copies, waits for them, and re-layouts, per_device(): row_density = jnp.take(density, gvec_cell, axis=2)  16.1 us
    another operation x1, local copies, waits for them, and re-layouts, per_device(): planes = jnp.stack([y_real, y_imag]).astype(jnp.bfloat16)  9.18 us
  transfers between devices with their start and end apart: 3, of which 2 were waited for; matrix products, arithmetic and copies ran while one was open for 3% of the time, Pallas kernels for 0%

commit v1 on v0

--- a/solution.py
+++ b/solution.py
@@ -121,7 +121,10 @@
         "jy,pxyk->pxjk", y_cosine, z_imag, precision=high
     )
     planes = jnp.stack([y_real, y_imag]).astype(jnp.bfloat16)
-    exchanged = lax.all_to_all(planes, "col", split_axis=3, concat_axis=2, tiled=True)
+    exchanged = jnp.concatenate(
+        lax.all_to_all(jnp.stack(jnp.split(planes, lax.axis_size("col"), axis=3)), "col", 0, 0),
+        axis=2,
+    )
     items = exchanged.shape[1]
     flat = exchanged.reshape(2, items, grid_x, -1)
     density = jnp.einsum(

time: 313 us -> 300 us (0.958)
  local copies, waits for them, and re-layouts: 97.1 us -> 90.4 us
  matrix products: 29.1 us -> 22.6 us
    reshape x2 -> x0, local copies, waits for them, and re-layouts: 17.8 us -> none  [per_device(): flat = exchanged.reshape(2, items, grid_x, -1)]
    another operation x1 -> x3, local copies, waits for them, and re-layouts: 9.18 us -> 20.3 us  [the longest x2 16.2 us: per_device(): flat = exchanged.reshape(2, items, grid_x, -1)]
    dot_general x1, matrix products: 7.89 us -> 4.61 us  [per_device(): z_real = jnp.einsum('kz,pxyz->pxyk', z_cosine, products, precision=high)]
    dot_general x1, matrix products: 5.43 us -> 2.25 us  [per_device(): z_imag = jnp.einsum('kz,pxyz->pxyk', z_sine, products, precision=high)]
  transfers between devices with their start and end apart: 3 -> 3, of which waited for: 2 -> 2; matrix products, arithmetic and copies ran while one was open for 3% -> 8% of each run, Pallas kernels for 0% -> 0%
where the time goes in v1:
time: 300 us; the launch traced here: 296 us
  waiting for transfers between devices  109 us (36%)
  local copies, waits for them, and re-layouts  90.4 us (30%)
  starting transfers between devices  35.6 us (12%)
  matrix products  22.6 us (8%)
  blocking collectives  21.5 us (7%)
  other arithmetic  15.6 us (5%)
    all_to_all x2, waiting for transfers between devices, copy_for_each(): lax.all_to_all(jnp.broadcast_to(x[None], (devices, *x.shape)), axis, 0, 0...  55.8 us
    all_to_all x1, waiting for transfers between devices, per_device(): lax.all_to_all(jnp.stack(jnp.split(planes, lax.axis_size('col'), axis=3))...  53.6 us
    reshape x1, local copies, waits for them, and re-layouts, per_device(): density = density.reshape(2, items, -1)  44.3 us
    all_to_all x2, starting transfers between devices, copy_for_each(): lax.all_to_all(jnp.broadcast_to(x[None], (devices, *x.shape)), axis, 0, 0...  28.3 us
    all_to_all x1, blocking collectives, sent_and_summed(): lax.all_to_all(pieces, axis, split_axis=0, concat_axis=0, tiled=True)  21.5 us
    another operation x2, local copies, waits for them, and re-layouts, per_device(): flat = exchanged.reshape(2, items, grid_x, -1)  16.2 us
    gather x1, local copies, waits for them, and re-layouts, per_device(): row_density = jnp.take(density, gvec_cell, axis=2)  16.1 us
    select_n x1, other arithmetic, per_device(): row_density = jnp.take(density, gvec_cell, axis=2)  7.45 us
  transfers between devices with their start and end apart: 3, of which 2 were waited for; matrix products, arithmetic and copies ran while one was open for 8% of the time, Pallas kernels for 0%

profile of v1, /device:TPU:2, one launch (start us, length us, event | category | flops | bytes accessed | tf_op | source)
XLA Modules:
  0.0 296.0 jit_solution(13399754177852298891)
XLA Ops:
  0.0 0.0 copy-start.1
  0.0 2.6 broadcast_in_dim.93
  2.6 9.6 %all-to-all-start = ((bf16[16,1,6,9216]{3,2,1,0:T(8,128)(2,1)}), bf16[16,1,6,9216]{3,2,1,0:T(8,128)(2,1)S(1)}, u32[]{:S(2)}, u32[]{:S(2)}) async-start(bf16[16,1,6,9216]{3,2,1,0:T(8,128)(2,1)} %broadcast_in_dim.93), calls=%async_computation | async-start | bytes 4718592 | tf_op jit(solution)/shard_map/all_to_all | solution.py:18
  12.2 0.0 copy-done.1
  12.2 55.8 %all-to-all-done = bf16[16,1,6,9216]{3,2,1,0:T(8,128)(2,1)S(1)} async-done(((bf16[16,1,6,9216]{3,2,1,0:T(8,128)(2,1)}), bf16[16,1,6,9216]{3,2,1,0:T(8,128)(2,1)S(1)}, u32[]{:S(2)}, u32[]{:S(2)}) %all-to-all-start) | async-done | bytes 1769504 | tf_op jit(solution)/shard_map/all_to_all | solution.py:18
  68.0 2.6 convert_multiply_fusion
  70.6 5.9 %reshape.292 = f32[16,6,96,96]{3,2,1,0:T(8,128)} reshape(f32[16,1,6,9216]{3,2,1,0:T(8,128)} %convert_multiply_fusion) | data formatting | bytes 7077888 | tf_op jit(solution)/shard_map/reshape | solution.py:114
  76.5 0.0 copy-start
  76.5 4.6 %fusion.35 = f32[16,6,96,96]{3,2,1,0:T(8,128)S(1)} fusion(f32[16,6,96,96]{3,2,1,0:T(8,128)} %reshape.292), kind=kOutput, calls=%fused_computation.95 | convolution fusion | flops 509690880 | bytes 7077888 | tf_op jit(solution)/shard_map/kz,pxyz->pxyk/dot_general | solution.py:115
  81.1 0.0 copy-done
  81.1 2.3 fusion.33
  83.4 2.3 fusion.38
  85.7 2.3 fusion.40
  88.0 2.7 fusion.6
  90.7 2.7 fusion.7
  93.5 0.3 bitcast_dynamic-update-slice_fusion.14
  93.8 0.2 bitcast_dynamic-update-slice_fusion.13
  94.0 0.2 bitcast_dynamic-update-slice_fusion.12
  94.2 0.2 bitcast_dynamic-update-slice_fusion.11
  94.4 0.1 bitcast_dynamic-update-slice_fusion.10
  94.5 0.2 bitcast_dynamic-update-slice_fusion.9
  94.7 0.2 bitcast_dynamic-update-slice_fusion.8
  94.9 0.2 bitcast_dynamic-update-slice_fusion.7
  95.1 0.1 bitcast_dynamic-update-slice_fusion.6
  95.2 0.2 bitcast_dynamic-update-slice_fusion.5
  95.4 0.2 bitcast_dynamic-update-slice_fusion.4
  95.6 0.2 bitcast_dynamic-update-slice_fusion.3
  95.8 0.1 bitcast_dynamic-update-slice_fusion.2
  95.9 0.2 bitcast_dynamic-update-slice_fusion.1
  96.1 0.2 bitcast_dynamic-update-slice_fusion
  96.3 0.2 fusion.26
  96.5 4.1 %copy.55 = bf16[16,2,16,6,6,96]{5,2,4,3,1,0:T(8,128)(2,1)} copy(bf16[16,2,16,6,6,96]{5,4,3,2,1,0:T(8,128)(2,1)S(1)} %fusion.26) | data formatting | bytes 7077888 | tf_op jit(solution)/shard_map/stack | solution.py:125
  100.5 0.0 copy-start.5
  100.6 0.0 copy-start.2
  100.6 7.3 %all-to-all-start.1 = ((bf16[16,2,16,6,6,96]{5,2,4,3,1,0:T(8,128)(2,1)}), bf16[16,2,16,6,6,96]{5,2,4,3,1,0:T(8,128)(2,1)}, u32[]{:S(2)}, u32[]{:S(2)}) async-start(bf16[16,2,16,6,6,96]{5,2,4,3,1,0:T(8,128)(2,1)} %copy.55), calls=%async_computation.1 | async-start | bytes 9437184 | tf_op jit(solution)/shard_map/all_to_all | solution.py:125
  108.6 0.0 copy-done.5
  108.6 0.0 copy-done.3
  108.6 0.0 copy-done.4
  108.6 0.2 select_reduce_fusion
  108.8 0.2 select_reduce_fusion.1
  109.0 0.0 copy-done.6
  109.0 0.2 select_reduce_fusion.2
  109.2 0.1 divide_multiply_fusion
  109.3 0.1 mul.268
  109.4 0.1 mul.269
  109.6 0.2 fusion.79
  109.8 0.2 multiply_convert_fusion
  110.1 0.0 copy-done.2
  110.1 53.6 %all-to-all-done.1 = bf16[16,2,16,6,6,96]{5,2,4,3,1,0:T(8,128)(2,1)} async-done(((bf16[16,2,16,6,6,96]{5,2,4,3,1,0:T(8,128)(2,1)}), bf16[16,2,16,6,6,96]{5,2,4,3,1,0:T(8,128)(2,1)}, u32[]{:S(2)}, u32[]{:S(2)}) %all-to-all-start.1) | async-done | bytes 3538976 | tf_op jit(solution)/shard_map/all_to_all | solution.py:125
  163.7 6.6 %copy.69 = bf16[2,16,16,6,6,96]{5,4,3,2,0,1:T(8,128)(2,1)} copy(bf16[2,16,16,6,6,96]{5,1,4,3,0,2:T(8,128)(2,1)} %bitcast.32) | data formatting | bytes 7077888 | tf_op jit(solution)/shard_map/reshape;reshape | solution.py:129
  170.3 9.6 %reshape.286 = bf16[2,16,96,576,1]{3,2,0,1,4:T(8,128)(2,1)} reshape(bf16[2,16,16,6,6,96]{5,4,3,2,0,1:T(8,128)(2,1)} %copy.69) | data formatting | bytes 7077888 | tf_op jit(solution)/shard_map/reshape;reshape | solution.py:129
  180.0 5.3 %fusion = bf16[2,16,96,576]{3,2,0,1:T(8,128)(2,1)} fusion(bf16[2,16,96,576,1]{3,2,0,1,4:T(8,128)(2,1)} %reshape.286, bf16[1,2,96,96]{3,2,1,0:T(8,128)(2,1)S(1)} %get-tuple-element.17, bf16[1,2,96,96]{3,2,1,0:T(8,128)(2,1)S(1)} %get-tuple-element.16), kind=kOutput, calls=%fused_computation.35 | convolution fusion | flops 681394176 | bytes 7151616 | tf_op jit(solution)/shard_map/orkx,rpxf->opkf/dot_general | solution.py:130
  185.3 44.3 %copy.72 = bf16[2,16,96,576]{1,0,3,2:T(2,128)(2,1)} copy(bf16[2,16,96,576]{3,2,0,1:T(8,128)(2,1)} %fusion) | data formatting | bytes 7077888 | tf_op jit(solution)/shard_map/reshape | solution.py:133
  229.5 0.7 fusion.83
  230.2 0.6 broadcast_in_dim.99
  230.8 18.7 %all-to-all-start.2 = ((bf16[16,2,16,1]{2,1,3,0:T(2,128)(2,1)}), bf16[16,2,16,1]{2,1,3,0:T(2,128)(2,1)S(1)}, u32[]{:S(2)}, u32[]{:S(2)}) async-start(bf16[16,2,16,1]{2,1,3,0:T(2,128)(2,1)} %broadcast_in_dim.99), calls=%async_computation.2 | async-start | bytes 16384 | tf_op jit(solution)/shard_map/all_to_all | solution.py:18
  249.5 16.1 %gather_fusion = bf16[2048,2,16]{2,1,0:T(2,128)(2,1)S(1)} fusion(bf16[2,16,55296]{1,0,2:T(2,128)(2,1)} %bitcast.124, s32[2048]{0:T(1024)S(1)} %fusion.82), kind=kCustom, calls=%fused_computation | custom fusion | bytes 270336 | tf_op jit(solution)/shard_map/jit(_take)/gather | solution.py:134
  265.6 7.5 %fusion.9 = bf16[2,16,2048]{1,0,2:T(2,128)(2,1)S(1)} fusion(bf16[2048,2,16]{2,1,0:T(2,128)(2,1)S(1)} %gather_fusion, pred[2048]{0:T(1024)(128)(4,1)S(1)} %compare_and_fusion), kind=kLoop, calls=%fused_computation.45 | loop fusion | flops 65536 | bytes 264192 | tf_op jit(solution)/shard_map/jit(_take)/select_n | solution.py:134
  273.0 0.0 all-to-all-done.2
  273.0 0.1 copy.60
  273.2 0.2 mul.261
  273.4 0.4 fusion.5
  273.8 21.5 %all_to_all.20 = bf16[16,128,128]{2,1,0:T(8,128)(2,1)S(1)} all-to-all(bf16[16,128,128]{2,1,0:T(8,128)(2,1)S(1)} %bitcast.125), channel_id=1, replica_groups=mesh['band'=16,'col'=16] {'band'}, dimensions={0} | all-to-all | bytes 1048576 | tf_op jit(solution)/shard_map/all_to_all | solution.py:33
  295.3 0.7 convert_reduce_fusion
  (16 shorter events, 0.2 us)
Async XLA Ops:
  0.0 12.2 %copy-start.1 = (bf16[1,6,9216]{2,1,0:T(8,128)(2,1)S(1)}, bf16[1,6,9216]{2,1,0:T(8,128)(2,1)}, u32[]{:S(2)}) copy-start(bf16[1,6,9216]{2,1,0:T(8,128)(2,1)} %param.9) | copy-start | bytes 331780
  2.6 65.4 %all-to-all-start = ((bf16[16,1,6,9216]{3,2,1,0:T(8,128)(2,1)}), bf16[16,1,6,9216]{3,2,1,0:T(8,128)(2,1)S(1)}, u32[]{:S(2)}, u32[]{:S(2)}) async-start(bf16[16,1,6,9216]{3,2,1,0:T(8,128)(2,1)} %broadcast_in_dim.93), calls=%async_computation | async-start | bytes 4718592 | tf_op jit(solution)/shard_map/all_to_all | solution.py:18
  76.5 4.6 %copy-start = (f32[16,6,96,96]{3,2,1,0:T(8,128)S(1)}, f32[16,6,96,96]{3,2,1,0:T(8,128)}, u32[]{:S(2)}) copy-start(f32[16,6,96,96]{3,2,1,0:T(8,128)} %reshape.292) | copy-start | bytes 10616836
  100.5 8.0 %copy-start.5 = (f32[4]{0:T(128)S(1)}, f32[4]{0:T(128)}, u32[]{:S(2)}) copy-start(f32[4]{0:T(128)} %param.13) | copy-start | bytes 52
  100.5 8.1 %copy-start.3 = (f32[4096]{0:T(1024)S(1)}, f32[4096]{0:T(1024)}, u32[]{:S(2)}) copy-start(f32[4096]{0:T(1024)} %param.11) | copy-start | bytes 49156
  100.5 8.1 %copy-start.4 = (s32[16]{0:T(128)S(1)}, s32[16]{0:T(128)}, u32[]{:S(2)}) copy-start(s32[16]{0:T(128)} %param.10) | copy-start | bytes 196
  100.5 8.5 %copy-start.6 = (f32[16]{0:T(128)S(1)}, f32[16]{0:T(128)}, u32[]{:S(2)}) copy-start(f32[16]{0:T(128)} %param.12) | copy-start | bytes 196
  100.6 9.5 %copy-start.2 = (s32[2048]{0:T(1024)S(1)}, s32[2048]{0:T(1024)}, u32[]{:S(2)}) copy-start(s32[2048]{0:T(1024)} %param.14) | copy-start | bytes 24580
  100.6 63.2 %all-to-all-start.1 = ((bf16[16,2,16,6,6,96]{5,2,4,3,1,0:T(8,128)(2,1)}), bf16[16,2,16,6,6,96]{5,2,4,3,1,0:T(8,128)(2,1)}, u32[]{:S(2)}, u32[]{:S(2)}) async-start(bf16[16,2,16,6,6,96]{5,2,4,3,1,0:T(8,128)(2,1)} %copy.55), calls=%async_computation.1 | async-start | bytes 9437184 | tf_op jit(solution)/shard_map/all_to_all | solution.py:125
  230.8 42.3 %all-to-all-start.2 = ((bf16[16,2,16,1]{2,1,3,0:T(2,128)(2,1)}), bf16[16,2,16,1]{2,1,3,0:T(2,128)(2,1)S(1)}, u32[]{:S(2)}, u32[]{:S(2)}) async-start(bf16[16,2,16,1]{2,1,3,0:T(2,128)(2,1)} %broadcast_in_dim.99), calls=%async_computation.2 | async-start | bytes 16384 | tf_op jit(solution)/shard_map/all_to_all | solution.py:18
